TPU v7x, 32 devices: a whole 2x2x4 slice. The times are simulated.
32 devices in a mesh: gx: 2 (over x), gy: 4 (over z), gz: 4 (over y, core).
Axes of the slice: x: 2, y: 2, z: 4, core: 2. Of those that a mesh axis runs over, the one named last changes fastest.
Arguments:
- local_displacement: float32 [2, 4, 4, 6, 128, 128], P('gx', 'gy', 'gz'), may hold values from -6 to 6
- coarse_load: float32 [2, 4, 4, 6, 128], P('gx', 'gy', 'gz'), may hold values from -12 to 12
- flexibility: float32 [2, 4, 4, 768, 768], P('gx', 'gy', 'gz'), as said below
- block_map: int32 [2, 4, 4, 768], P('gx', 'gy', 'gz'), may hold values from 0 to 767, each once within a row
- mode_counts: int32 [2, 4, 4], P('gx', 'gy', 'gz'), may hold values from 3 to 6, as said below
- mode_traces: float32 [2, 4, 4, 6, 6, 128], P('gx', 'gy', 'gz')
- coarse_rows: float32 [2, 4, 4, 6, 192], P('gx', 'gy', 'gz'), as said below
- stored_dirs: float32 [2, 4, 4, 40, 6, 128], P('gx', 'gy', 'gz'), as said below
- stored_images: float32 [2, 4, 4, 40, 6, 128], P('gx', 'gy', 'gz'), as said below
- stored_curv: float32 [40], replicated, may hold values from 1 to 4
Outputs:
- multipliers: float32 [2, 4, 4, 6, 128, 128], P('gx', 'gy', 'gz')
- residual: float32 [2, 4, 4, 6, 128, 128], P('gx', 'gy', 'gz')
Inputs may be any that keep to these rules, and one draw needn't show every extreme that they name: `flexibility`: each subdomain's matrix is symmetric positive definite. `coarse_rows`: read as a [192, 192] matrix it is exactly symmetric: the inverse of G^T G for the coarse basis G of the present modes, with ones added on the diagonal of absent modes. `mode_counts`: modes numbered from the count on are absent. `block_map`: each subdomain's row names every interface position once. `stored_dirs`: both copies of every face agree: slot 2a of a subdomain equals slot 2a+1 of its lower neighbour along grid dimension a. `stored_images`: both copies of every face agree: slot 2a of a subdomain equals slot 2a+1 of its lower neighbour along grid dimension a.
All inputs are finite; a program needn't handle non-finite values.
Results may differ from a plain program's by a relative error of at most 0.0003.
Values sent between devices are 32-bit elements; how exact they have to be, the bound alone decides.
A program may use at most 128 MiB of HBM per device.

v0:
```python
import jax
import jax.numpy as jnp
from jax import lax
from jax.sharding import PartitionSpec as P

STORED = 40
ITERS = 3


precise = lax.Precision.HIGHEST
slot_signs = (-1.0, 1.0, -1.0, 1.0, -1.0, 1.0)


def extended(x, sides, width):
    for axis, dim in sides:
        peers, length = (lax.axis_size(axis), x.shape[dim])
        up = [(i, (i + 1) % peers) for i in range(peers)]
        down = [(j, i) for i, j in up]
        last = lax.slice_in_dim(x, length - width, length, axis=dim)
        initial = lax.slice_in_dim(x, 0, width, axis=dim)
        before = lax.ppermute(last, axis, up)
        after = lax.ppermute(initial, axis, down)
        x = jnp.concatenate([before, x, after], axis=dim)
    return x


def assemble(field):
    padded_x = extended(field[0:2], (("gx", 0),), 1)
    padded_y = extended(field[2:4], (("gy", 0),), 1)
    padded_z = extended(field[4:6], (("gz", 0),), 1)
    return jnp.stack(
        [
            field[0] + padded_x[0],
            field[1] + padded_x[3],
            field[2] + padded_y[0],
            field[3] + padded_y[3],
            field[4] + padded_z[0],
            field[5] + padded_z[3],
        ]
    )


def plus_inner(first, second):
    return jnp.sum(first[1::2] * second[1::2], axis=(0, 1))


def stored_inner(store, field):
    return jnp.einsum("isf,sfr->ir", store[:, 1::2], field[1::2], precision=precise)


def coarse_solve(loads, rows):
    return jnp.dot(
        rows, lax.all_gather(loads, ("gx", "gy", "gz"), axis=0, tiled=True), precision=precise
    )


def per_device(
    local_displacement,
    coarse_load,
    flexibility,
    block_map,
    mode_counts,
    mode_traces,
    coarse_rows,
    stored_dirs,
    stored_images,
    stored_curv,
):
    displacement = local_displacement[0, 0, 0]
    loads = coarse_load[0, 0, 0]
    flex = flexibility[0, 0, 0]
    mapping = block_map[0, 0, 0]
    rows = coarse_rows[0, 0, 0]
    dirs_store = stored_dirs[0, 0, 0]
    images_store = stored_images[0, 0, 0]
    signs = jnp.array(slot_signs, jnp.float32)
    field_signs = signs[:, None, None]
    nmodes = mode_traces.shape[3]
    present = (jnp.arange(nmodes, dtype=jnp.int32) < mode_counts[0, 0, 0]).astype(jnp.float32)
    signed = mode_traces[0, 0, 0] * present[:, None, None] * signs[None, :, None]
    size_nb = flex.shape[0]
    inverse = jnp.zeros((size_nb,), jnp.int32).at[mapping].set(jnp.arange(size_nb, dtype=jnp.int32))
    flex_face = jnp.take(jnp.take(flex, inverse, axis=0), inverse, axis=1)
    layout = displacement.shape

    def operate(field):
        flat = (field_signs * field).reshape(size_nb, layout[2])
        return jnp.dot(flex_face, flat, precision=precise).reshape(layout)

    def graph(alpha):
        return assemble(jnp.einsum("msf,mr->sfr", signed, alpha, precision=precise))

    def project(field):
        partial_loads = jnp.einsum("msf,sfr->mr", signed, field, precision=precise)
        return field - graph(coarse_solve(partial_loads, rows))

    lam = graph(coarse_solve(loads, rows))
    resid = project(assemble(field_signs * (displacement - operate(lam))))
    directions, images, curves = ([], [], [])
    for step in range(ITERS):
        local_rows = stored_inner(images_store, resid)
        if images:
            own_rows = jnp.stack([plus_inner(images[index], resid) for index in range(len(images))])
            local_rows = jnp.concatenate([local_rows, own_rows], axis=0)
        totals = lax.psum(local_rows, ("gx", "gy", "gz"))
        beta = totals[:STORED] / stored_curv[:, None]
        direction = resid - jnp.einsum("isf,ir->sfr", dirs_store, beta, precision=precise)
        for index in range(len(directions)):
            direction = direction - directions[index] * (totals[STORED + index] / curves[index])
        image_now = project(assemble(field_signs * operate(direction)))
        pair = lax.psum(
            jnp.stack([plus_inner(direction, image_now), plus_inner(direction, resid)]),
            ("gx", "gy", "gz"),
        )
        rate = pair[1] / pair[0]
        lam = lam + rate * direction
        resid = resid - rate * image_now
        directions.append(direction)
        images.append(image_now)
        curves.append(pair[0])
    return (lam[None, None, None], resid[None, None, None])


def solution(mesh):
    return jax.shard_map(
        per_device,
        mesh=mesh,
        in_specs=(
            P("gx", "gy", "gz", None, None, None),
            P("gx", "gy", "gz", None, None),
            P("gx", "gy", "gz", None, None),
            P("gx", "gy", "gz", None),
            P("gx", "gy", "gz"),
            P("gx", "gy", "gz", None, None, None),
            P("gx", "gy", "gz", None, None),
            P("gx", "gy", "gz", None, None, None),
            P("gx", "gy", "gz", None, None, None),
            P(),
        ),
        out_specs=(P("gx", "gy", "gz", None, None, None), P("gx", "gy", "gz", None, None, None)),
        check_vma=False,
    )
```

profile of v0, /device:TPU:0, one launch (start us, length us, event | category | flops | bytes accessed | tf_op | source)
XLA Modules:
  0.0 665.4 jit_solution(9631356648595068276)
XLA Ops:
  1.5 43.8 %all-gather = f32[1,1,1,192,128]{4,2,1,0,3:T(1,128)S(1)} all-gather(f32[1,1,1,6,128]{4,2,1,0,3:T(1,128)} %bitcast.275), channel_id=2, replica_groups=mesh['gx'=2,'gy'=4,'gz'=4] {'gx','gy','gz'}, dimensions={3}, use_global_device_ids=true | all-gather | bytes 101376 | tf_op jit(solution)/shard_map/all_gather | solution.py:53
  62.3 5.8 gather_fusion.1
  77.4 3.8 collective-permute-start.3
  84.9 3.7 fusion.4
  89.3 3.7 collective-permute-done.6
  93.6 3.8 collective-permute-start.9
  102.9 39.0 %all-gather.1 = f32[32,6,128]{2,1,0:T(8,128)S(1)} all-gather(f32[1,6,128]{2,1,0:T(8,128)S(1)} %convolution_bitcast_fusion.14), channel_id=1, replica_groups=mesh['gx'=2,'gy'=4,'gz'=4] {'gx','gy','gz'}, dimensions={0}, use_global_device_ids=true | all-gather | bytes 101376 | tf_op jit(solution)/shard_map/all_gather | solution.py:53
  148.3 3.8 collective-permute-start.15
  158.5 37.8 %psum.42 = f32[40,128]{1,0:T(8,128)} all-reduce(f32[40,128]{1,0:T(8,128)S(1)} %convolution_bitcast_fusion.5), channel_id=1, replica_groups=mesh['gx'=2,'gy'=4,'gz'=4] {'gx','gy','gz'}, use_global_device_ids=true, to_apply=%region_1.2 | all-reduce | flops 5120 | bytes 40960 | tf_op jit(solution)/shard_map/psum | solution.py:105
  216.2 43.3 %all-gather.2 = f32[32,6,128]{2,1,0:T(8,128)} all-gather(f32[1,6,128]{2,1,0:T(8,128)S(1)} %convolution_bitcast_fusion.13), channel_id=1, replica_groups=mesh['gx'=2,'gy'=4,'gz'=4] {'gx','gy','gz'}, dimensions={0}, use_global_device_ids=true | all-gather | bytes 101376 | tf_op jit(solution)/shard_map/all_gather | solution.py:53
  272.7 3.8 collective-permute-start.27
  283.5 37.2 %psum.43 = f32[2,128]{1,0:T(2,128)S(1)} all-reduce(f32[2,128]{1,0:T(2,128)S(1)} %pad_maximum_fusion.2), channel_id=1, replica_groups=mesh['gx'=2,'gy'=4,'gz'=4] {'gx','gy','gz'}, use_global_device_ids=true, to_apply=%region_4.5 | all-reduce | flops 256 | bytes 2048 | tf_op jit(solution)/shard_map/psum | solution.py:111
  324.4 41.8 %psum.44 = f32[41,128]{1,0:T(8,128)S(1)} all-reduce(f32[41,128]{1,0:T(8,128)S(1)} %pad_maximum_fusion), channel_id=1, replica_groups=mesh['gx'=2,'gy'=4,'gz'=4] {'gx','gy','gz'}, use_global_device_ids=true, to_apply=%region_6.7 | all-reduce | flops 5248 | bytes 41984 | tf_op jit(solution)/shard_map/psum | solution.py:105
  369.4 3.7 convolution_multiply_fusion.1
  378.3 3.8 collective-permute-start.33
  387.6 40.3 %all-gather.3 = f32[32,6,128]{2,1,0:T(8,128)S(1)} all-gather(f32[1,6,128]{2,1,0:T(8,128)S(1)} %convolution_bitcast_fusion.12), channel_id=1, replica_groups=mesh['gx'=2,'gy'=4,'gz'=4] {'gx','gy','gz'}, dimensions={0}, use_global_device_ids=true | all-gather | bytes 101376 | tf_op jit(solution)/shard_map/all_gather | solution.py:53
  438.6 3.8 collective-permute-start.39
  449.9 37.4 %psum.45 = f32[2,128]{1,0:T(2,128)} all-reduce(f32[2,128]{1,0:T(2,128)} %pad_maximum_fusion.3), channel_id=1, replica_groups=mesh['gx'=2,'gy'=4,'gz'=4] {'gx','gy','gz'}, use_global_device_ids=true, to_apply=%region_9.10 | all-reduce | flops 256 | bytes 2048 | tf_op jit(solution)/shard_map/psum | solution.py:111
  491.5 42.2 %psum.46 = f32[42,128]{1,0:T(8,128)S(1)} all-reduce(f32[42,128]{1,0:T(8,128)S(1)} %pad_maximum_fusion.1), channel_id=1, replica_groups=mesh['gx'=2,'gy'=4,'gz'=4] {'gx','gy','gz'}, use_global_device_ids=true, to_apply=%region_12.13 | all-reduce | flops 5376 | bytes 43008 | tf_op jit(solution)/shard_map/psum | solution.py:105
  537.3 3.7 convolution_multiply_fusion
  546.2 3.8 collective-permute-start.45
  555.7 39.9 %all-gather.4 = f32[32,6,128]{2,1,0:T(8,128)S(1)} all-gather(f32[1,6,128]{2,1,0:T(8,128)S(1)} %convolution_bitcast_fusion.11), channel_id=1, replica_groups=mesh['gx'=2,'gy'=4,'gz'=4] {'gx','gy','gz'}, dimensions={0}, use_global_device_ids=true | all-gather | bytes 101376 | tf_op jit(solution)/shard_map/all_gather | solution.py:53
  606.6 3.8 collective-permute-start.51
  616.6 37.2 %psum.47 = f32[2,128]{1,0:T(2,128)S(1)} all-reduce(f32[2,128]{1,0:T(2,128)S(1)} %pad_maximum_fusion.4), channel_id=1, replica_groups=mesh['gx'=2,'gy'=4,'gz'=4] {'gx','gy','gz'}, use_global_device_ids=true, to_apply=%region_15.16 | all-reduce | flops 256 | bytes 2048 | tf_op jit(solution)/shard_map/psum | solution.py:111
  (464 shorter events, 171.1 us)
Async XLA Ops:
  47.7 20.3 %collective-permute-start = (f32[1,128,128]{2,1,0:T(8,128)S(1)}, f32[1,128,128]{2,1,0:T(8,128)}, u32[]{:S(2)}, u32[]{:S(2)}) collective-permute-start(f32[1,128,128]{2,1,0:T(8,128)S(1)} %slice.456), channel_id=1, source_target_pairs={{0,16},{16,0},{1,17},{17,1},{2,18},{18,2},{3,19},{19,3},{4,20},{20... | collective-permute-start | bytes 196616 | tf_op jit(solution)/shard_map/ppermute | solution.py:21
  68.9 12.3 %collective-permute-start.1 = (f32[1,128,128]{2,1,0:T(8,128)S(1)}, f32[1,128,128]{2,1,0:T(8,128)}, u32[]{:S(2)}, u32[]{:S(2)}) collective-permute-start(f32[1,128,128]{2,1,0:T(8,128)S(1)} %get-tuple-element.63), channel_id=1, source_target_pairs={{16,0},{0,16},{17,1},{1,17},{18,2},{2,18},{19,3},{3,19},{20,4},{4,... | collective-permute-start | bytes 196616 | tf_op jit(solution)/shard_map/ppermute | solution.py:22
  93.0 8.8 %collective-permute-start.11 = (f32[1,128,128]{2,1,0:T(8,128)S(1)}, f32[1,128,128]{2,1,0:T(8,128)S(1)}, u32[]{:S(2)}, u32[]{:S(2)}) collective-permute-start(f32[1,128,128]{2,1,0:T(8,128)S(1)} %get-tuple-element.52), channel_id=1, source_target_pairs={{1,0},{2,1},{3,2},{0,3},{5,4},{6,5},{7,6},{4,7},{9,8},{10,9},{11,1... | collective-permute-start | bytes 196616 | tf_op jit(solution)/shard_map/ppermute | solution.py:22
  93.1 8.7 %collective-permute-start.10 = (f32[1,128,128]{2,1,0:T(8,128)S(1)}, f32[1,128,128]{2,1,0:T(8,128)S(1)}, u32[]{:S(2)}, u32[]{:S(2)}) collective-permute-start(f32[1,128,128]{2,1,0:T(8,128)S(1)} %get-tuple-element.54), channel_id=1, source_target_pairs={{0,1},{1,2},{2,3},{3,0},{4,5},{5,6},{6,7},{7,4},{8,9},{9,10},{10,1... | collective-permute-start | bytes 196616 | tf_op jit(solution)/shard_map/ppermute | solution.py:21
  147.7 9.3 %collective-permute-start.17 = (f32[1,128,128]{2,1,0:T(8,128)S(1)}, f32[1,128,128]{2,1,0:T(8,128)S(1)}, u32[]{:S(2)}, u32[]{:S(2)}) collective-permute-start(f32[1,128,128]{2,1,0:T(8,128)S(1)} %get-tuple-element.46), channel_id=1, source_target_pairs={{1,0},{2,1},{3,2},{0,3},{5,4},{6,5},{7,6},{4,7},{9,8},{10,9},{11,1... | collective-permute-start | bytes 196616 | tf_op jit(solution)/shard_map/ppermute | solution.py:22
  147.8 9.2 %collective-permute-start.16 = (f32[1,128,128]{2,1,0:T(8,128)S(1)}, f32[1,128,128]{2,1,0:T(8,128)S(1)}, u32[]{:S(2)}, u32[]{:S(2)}) collective-permute-start(f32[1,128,128]{2,1,0:T(8,128)S(1)} %get-tuple-element.48), channel_id=1, source_target_pairs={{0,1},{1,2},{2,3},{3,0},{4,5},{5,6},{6,7},{7,4},{8,9},{9,10},{10,1... | collective-permute-start | bytes 196616 | tf_op jit(solution)/shard_map/ppermute | solution.py:21
  148.3 8.6 %collective-permute-start.15 = (f32[1,128,128]{2,1,0:T(8,128)S(1)}, f32[1,128,128]{2,1,0:T(8,128)S(1)}, u32[]{:S(2)}, u32[]{:S(2)}) collective-permute-start(f32[1,128,128]{2,1,0:T(8,128)S(1)} %get-tuple-element.50), channel_id=1, source_target_pairs={{4,0},{8,4},{12,8},{0,12},{5,1},{9,5},{13,9},{1,13},{6,2},{10,6},{... | collective-permute-start | bytes 196616 | tf_op jit(solution)/shard_map/ppermute | solution.py:22
  206.5 9.0 %collective-permute-start.23 = (f32[1,128,128]{2,1,0:T(8,128)S(1)}, f32[1,128,128]{2,1,0:T(8,128)S(1)}, u32[]{:S(2)}, u32[]{:S(2)}) collective-permute-start(f32[1,128,128]{2,1,0:T(8,128)S(1)} %get-tuple-element.40), channel_id=1, source_target_pairs={{1,0},{2,1},{3,2},{0,3},{5,4},{6,5},{7,6},{4,7},{9,8},{10,9},{11,1... | collective-permute-start | bytes 196616 | tf_op jit(solution)/shard_map/ppermute | solution.py:22
  206.6 8.9 %collective-permute-start.22 = (f32[1,128,128]{2,1,0:T(8,128)S(1)}, f32[1,128,128]{2,1,0:T(8,128)S(1)}, u32[]{:S(2)}, u32[]{:S(2)}) collective-permute-start(f32[1,128,128]{2,1,0:T(8,128)S(1)} %get-tuple-element.42), channel_id=1, source_target_pairs={{0,1},{1,2},{2,3},{3,0},{4,5},{5,6},{6,7},{7,4},{8,9},{9,10},{10,1... | collective-permute-start | bytes 196616 | tf_op jit(solution)/shard_map/ppermute | solution.py:21
  272.1 9.3 %collective-permute-start.29 = (f32[1,128,128]{2,1,0:T(8,128)S(1)}, f32[1,128,128]{2,1,0:T(8,128)S(1)}, u32[]{:S(2)}, u32[]{:S(2)}) collective-permute-start(f32[1,128,128]{2,1,0:T(8,128)S(1)} %get-tuple-element.34), channel_id=1, source_target_pairs={{1,0},{2,1},{3,2},{0,3},{5,4},{6,5},{7,6},{4,7},{9,8},{10,9},{11,1... | collective-permute-start | bytes 196616 | tf_op jit(solution)/shard_map/ppermute | solution.py:22
  272.2 9.2 %collective-permute-start.28 = (f32[1,128,128]{2,1,0:T(8,128)S(1)}, f32[1,128,128]{2,1,0:T(8,128)S(1)}, u32[]{:S(2)}, u32[]{:S(2)}) collective-permute-start(f32[1,128,128]{2,1,0:T(8,128)S(1)} %get-tuple-element.36), channel_id=1, source_target_pairs={{0,1},{1,2},{2,3},{3,0},{4,5},{5,6},{6,7},{7,4},{8,9},{9,10},{10,1... | collective-permute-start | bytes 196616 | tf_op jit(solution)/shard_map/ppermute | solution.py:21
  272.7 8.6 %collective-permute-start.27 = (f32[1,128,128]{2,1,0:T(8,128)S(1)}, f32[1,128,128]{2,1,0:T(8,128)S(1)}, u32[]{:S(2)}, u32[]{:S(2)}) collective-permute-start(f32[1,128,128]{2,1,0:T(8,128)S(1)} %get-tuple-element.38), channel_id=1, source_target_pairs={{4,0},{8,4},{12,8},{0,12},{5,1},{9,5},{13,9},{1,13},{6,2},{10,6},{... | collective-permute-start | bytes 196616 | tf_op jit(solution)/shard_map/ppermute | solution.py:22
  377.8 9.1 %collective-permute-start.35 = (f32[1,128,128]{2,1,0:T(8,128)S(1)}, f32[1,128,128]{2,1,0:T(8,128)S(1)}, u32[]{:S(2)}, u32[]{:S(2)}) collective-permute-start(f32[1,128,128]{2,1,0:T(8,128)S(1)} %get-tuple-element.28), channel_id=1, source_target_pairs={{1,0},{2,1},{3,2},{0,3},{5,4},{6,5},{7,6},{4,7},{9,8},{10,9},{11,1... | collective-permute-start | bytes 196616 | tf_op jit(solution)/shard_map/ppermute | solution.py:22
  377.8 9.0 %collective-permute-start.34 = (f32[1,128,128]{2,1,0:T(8,128)S(1)}, f32[1,128,128]{2,1,0:T(8,128)S(1)}, u32[]{:S(2)}, u32[]{:S(2)}) collective-permute-start(f32[1,128,128]{2,1,0:T(8,128)S(1)} %get-tuple-element.30), channel_id=1, source_target_pairs={{0,1},{1,2},{2,3},{3,0},{4,5},{5,6},{6,7},{7,4},{8,9},{9,10},{10,1... | collective-permute-start | bytes 196616 | tf_op jit(solution)/shard_map/ppermute | solution.py:21
  438.1 9.3 %collective-permute-start.41 = (f32[1,128,128]{2,1,0:T(8,128)S(1)}, f32[1,128,128]{2,1,0:T(8,128)S(1)}, u32[]{:S(2)}, u32[]{:S(2)}) collective-permute-start(f32[1,128,128]{2,1,0:T(8,128)S(1)} %get-tuple-element.22), channel_id=1, source_target_pairs={{1,0},{2,1},{3,2},{0,3},{5,4},{6,5},{7,6},{4,7},{9,8},{10,9},{11,1... | collective-permute-start | bytes 196616 | tf_op jit(solution)/shard_map/ppermute | solution.py:22
  438.1 9.2 %collective-permute-start.40 = (f32[1,128,128]{2,1,0:T(8,128)S(1)}, f32[1,128,128]{2,1,0:T(8,128)S(1)}, u32[]{:S(2)}, u32[]{:S(2)}) collective-permute-start(f32[1,128,128]{2,1,0:T(8,128)S(1)} %get-tuple-element.24), channel_id=1, source_target_pairs={{0,1},{1,2},{2,3},{3,0},{4,5},{5,6},{6,7},{7,4},{8,9},{9,10},{10,1... | collective-permute-start | bytes 196616 | tf_op jit(solution)/shard_map/ppermute | solution.py:21
  438.6 8.6 %collective-permute-start.39 = (f32[1,128,128]{2,1,0:T(8,128)S(1)}, f32[1,128,128]{2,1,0:T(8,128)S(1)}, u32[]{:S(2)}, u32[]{:S(2)}) collective-permute-start(f32[1,128,128]{2,1,0:T(8,128)S(1)} %get-tuple-element.26), channel_id=1, source_target_pairs={{4,0},{8,4},{12,8},{0,12},{5,1},{9,5},{13,9},{1,13},{6,2},{10,6},{... | collective-permute-start | bytes 196616 | tf_op jit(solution)/shard_map/ppermute | solution.py:22
  545.6 9.3 %collective-permute-start.47 = (f32[1,128,128]{2,1,0:T(8,128)S(1)}, f32[1,128,128]{2,1,0:T(8,128)S(1)}, u32[]{:S(2)}, u32[]{:S(2)}) collective-permute-start(f32[1,128,128]{2,1,0:T(8,128)S(1)} %get-tuple-element.16), channel_id=1, source_target_pairs={{1,0},{2,1},{3,2},{0,3},{5,4},{6,5},{7,6},{4,7},{9,8},{10,9},{11,1... | collective-permute-start | bytes 196616 | tf_op jit(solution)/shard_map/ppermute | solution.py:22
  545.7 9.2 %collective-permute-start.46 = (f32[1,128,128]{2,1,0:T(8,128)S(1)}, f32[1,128,128]{2,1,0:T(8,128)S(1)}, u32[]{:S(2)}, u32[]{:S(2)}) collective-permute-start(f32[1,128,128]{2,1,0:T(8,128)S(1)} %get-tuple-element.18), channel_id=1, source_target_pairs={{0,1},{1,2},{2,3},{3,0},{4,5},{5,6},{6,7},{7,4},{8,9},{9,10},{10,1... | collective-permute-start | bytes 196616 | tf_op jit(solution)/shard_map/ppermute | solution.py:21
  546.2 8.6 %collective-permute-start.44 = (f32[1,128,128]{2,1,0:T(8,128)S(1)}, f32[1,128,128]{2,1,0:T(8,128)S(1)}, u32[]{:S(2)}, u32[]{:S(2)}) collective-permute-start(f32[1,128,128]{2,1,0:T(8,128)S(1)} %get-tuple-element.19), channel_id=1, source_target_pairs={{0,4},{4,8},{8,12},{12,0},{1,5},{5,9},{9,13},{13,1},{2,6},{6,10},{... | collective-permute-start | bytes 196616 | tf_op jit(solution)/shard_map/ppermute | solution.py:21
  546.2 8.7 %collective-permute-start.45 = (f32[1,128,128]{2,1,0:T(8,128)S(1)}, f32[1,128,128]{2,1,0:T(8,128)S(1)}, u32[]{:S(2)}, u32[]{:S(2)}) collective-permute-start(f32[1,128,128]{2,1,0:T(8,128)S(1)} %get-tuple-element.20), channel_id=1, source_target_pairs={{4,0},{8,4},{12,8},{0,12},{5,1},{9,5},{13,9},{1,13},{6,2},{10,6},{... | collective-permute-start | bytes 196616 | tf_op jit(solution)/shard_map/ppermute | solution.py:22
  606.0 9.3 %collective-permute-start.53 = (f32[1,128,128]{2,1,0:T(8,128)S(1)}, f32[1,128,128]{2,1,0:T(8,128)S(1)}, u32[]{:S(2)}, u32[]{:S(2)}) collective-permute-start(f32[1,128,128]{2,1,0:T(8,128)S(1)} %get-tuple-element.10), channel_id=1, source_target_pairs={{1,0},{2,1},{3,2},{0,3},{5,4},{6,5},{7,6},{4,7},{9,8},{10,9},{11,1... | collective-permute-start | bytes 196616 | tf_op jit(solution)/shard_map/ppermute | solution.py:22
  606.1 9.2 %collective-permute-start.52 = (f32[1,128,128]{2,1,0:T(8,128)S(1)}, f32[1,128,128]{2,1,0:T(8,128)S(1)}, u32[]{:S(2)}, u32[]{:S(2)}) collective-permute-start(f32[1,128,128]{2,1,0:T(8,128)S(1)} %get-tuple-element.12), channel_id=1, source_target_pairs={{0,1},{1,2},{2,3},{3,0},{4,5},{5,6},{6,7},{7,4},{8,9},{9,10},{10,1... | collective-permute-start | bytes 196616 | tf_op jit(solution)/shard_map/ppermute | solution.py:21
  606.6 8.6 %collective-permute-start.51 = (f32[1,128,128]{2,1,0:T(8,128)S(1)}, f32[1,128,128]{2,1,0:T(8,128)S(1)}, u32[]{:S(2)}, u32[]{:S(2)}) collective-permute-start(f32[1,128,128]{2,1,0:T(8,128)S(1)} %get-tuple-element.14), channel_id=1, source_target_pairs={{4,0},{8,4},{12,8},{0,12},{5,1},{9,5},{13,9},{1,13},{6,2},{10,6},{... | collective-permute-start | bytes 196616 | tf_op jit(solution)/shard_map/ppermute | solution.py:22
  (126 other events, 1162.2 us)
where the time goes:
time: 668 us; the launch traced here: 665 us
  blocking collectives  440 us (66%)
  starting transfers between devices  64.8 us (10%)
  other arithmetic  60.4 us (9%)
  matrix products  34.5 us (5%)
  waiting for transfers between devices  32.7 us (5%)
  local copies, waits for them, and re-layouts  29.8 us (4%)
    all_gather x5, blocking collectives, coarse_solve(): lax.all_gather(loads, ('gx', 'gy', 'gz'), axis=0, tiled=True)  206 us
    psum x3, blocking collectives, per_device(): totals = lax.psum(local_rows, ('gx', 'gy', 'gz'))  122 us
    psum x3, blocking collectives, per_device(): lax.psum(jnp.stack([plus_inner(direction, image_now), plus_inner(directio...  112 us
    ppermute x27, starting transfers between devices, extended(): after = lax.ppermute(initial, axis, down)  45.3 us
    unnamed x76, other arithmetic  32.8 us
    ppermute x27, waiting for transfers between devices, extended(): after = lax.ppermute(initial, axis, down)  20.6 us
    ppermute x27, starting transfers between devices, extended(): before = lax.ppermute(last, axis, up)  19.5 us
    dot_general x4, matrix products, operate(): return jnp.dot(flex_face, flat, precision=precise).reshape(layout)  14.8 us
  transfers between devices with their start and end apart: 54, of which 13 were waited for; matrix products, arithmetic and copies ran while one was open for 9% of the time, Pallas kernels for 0%

commit v1 on v0

--- a/solution.py
+++ b/solution.py
@@ -1,14 +1,340 @@
+import functools
+
 import jax
 import jax.numpy as jnp
 from jax import lax
+from jax.experimental import pallas as pl
+from jax.experimental.pallas import tpu as pltpu
 from jax.sharding import PartitionSpec as P
 
-STORED = 40
 ITERS = 3
-
-
-precise = lax.Precision.HIGHEST
-slot_signs = (-1.0, 1.0, -1.0, 1.0, -1.0, 1.0)
+AXES = ("gx", "gy", "gz")
+F32 = jnp.float32
+BF16 = jnp.bfloat16
+MESH = pl.DeviceIdType.MESH
+
+
+def up_to(value, step):
+    return -(-value // step) * step
+
+
+def mm(a, b, ca=1, cb=0):
+    return lax.dot_general(a, b, (((ca,), (cb,)), ((), ())), preferred_element_type=F32)
+
+
+def mmf(a, b, ca=1, cb=0):
+    return lax.dot_general(
+        a, b, (((ca,), (cb,)), ((), ())), precision=lax.Precision.HIGHEST, preferred_element_type=F32
+    )
+
+
+def split(x):
+    hi = x.astype(BF16)
+    return hi, (x - hi.astype(F32)).astype(BF16)
+
+
+def pair(x):
+    hi, lo = split(x)
+    return jnp.concatenate([hi, lo], axis=1), hi
+
+
+def dot3(hi, lo, packed, xhi):
+    wide = mm(hi, packed)
+    width = xhi.shape[1]
+    return wide[:, :width] + wide[:, width:] + mm(lo, xhi)
+
+
+def colsum(x):
+    return jnp.sum(x, axis=0, keepdims=True)
+
+
+def kernel(
+    sizes,
+    disp, small, flex, bmap, cnt, traces, dirs, images, curv,
+    lam, w,
+    perm, a_hi, a_lo, m_hi, m_lo, xd_hi, xd_lo, z_hi, z_lo, tm, t_hi, t_lo,
+    g_src, g_dst, nm_src, nm_dst, hbuf, fbuf, ybuf, rs_src, rs_dst, bc_src, bc_dst,
+    pbuf, qbuf, vbuf,
+    g_ss, g_rs, nm_ss, nm_rs, f_ss, f_rs, rs_ss, rs_rs, bc_ss, bc_rs,
+):
+    nx, ny, nz = sizes
+    n = nx * ny * nz
+    slots, face, rhs = disp.shape
+    nb = slots * face
+    stored = dirs.shape[0]
+    modes = traces.shape[0]
+    mp = tm.shape[0]
+    npad = n * mp
+    koff = up_to(stored, 8)
+    kw = xd_hi.shape[1]
+    chunk = rs_src.shape[1]
+    cx, cy, cz = (lax.axis_index(a) for a in AXES)
+    me = (cx * ny + cy) * nz + cz
+
+    def coords(e):
+        return (e // (ny * nz), (e // nz) % ny, e % nz)
+
+    def neighbour(slot):
+        c = [cx, cy, cz]
+        a = slot // 2
+        step = sizes[a] - 1 if slot % 2 == 0 else 1
+        c[a] = lax.rem(c[a] + step, sizes[a])
+        return tuple(c)
+
+    def linear(c):
+        return (c[0] * ny + c[1]) * nz + c[2]
+
+    def sl(s):
+        return slice(s * face, (s + 1) * face)
+
+    def peers(body):
+        def step(r, carry):
+            body(lax.rem(me + r, n))
+            return carry
+        lax.fori_loop(1, n, step, 0)
+
+    def to_peer(src, dst, ss, rs, e):
+        return pltpu.make_async_remote_copy(
+            src_ref=src, dst_ref=dst.at[me], send_sem=ss.at[e], recv_sem=rs.at[me],
+            device_id=coords(e), device_id_type=MESH)
+
+    def from_peer(src, dst, ss, rs, e):
+        return pltpu.make_async_remote_copy(
+            src_ref=src, dst_ref=dst.at[e], send_sem=ss.at[e], recv_sem=rs.at[e],
+            device_id=coords(e), device_id_type=MESH)
+
+    def to_face(src, dst, ss, rs, s):
+        return pltpu.make_async_remote_copy(
+            src_ref=src.at[s], dst_ref=dst.at[s ^ 1], send_sem=ss.at[s], recv_sem=rs.at[s ^ 1],
+            device_id=neighbour(s), device_id_type=MESH)
+
+    barrier = pltpu.get_barrier_semaphore()
+    peers(lambda e: pl.semaphore_signal(barrier, inc=1, device_id=coords(e), device_id_type=MESH))
+
+    signs = [-1.0, 1.0] * (slots // 2)
+    present = (lax.broadcasted_iota(jnp.int32, (modes, face), 0) < cnt[0]).astype(F32)
+    tm[...] = jnp.zeros_like(tm)
+    nm_src[...] = jnp.zeros_like(nm_src)
+    g_src[:, npad + rhs:] = jnp.zeros((mp, kw), F32)
+    g_src[:, :npad + rhs] = small[...]
+    kz = jnp.zeros((mp, koff), F32)
+    kd = jnp.zeros((mp, koff), F32)
+    zero_rows = jnp.zeros((koff - stored, face), F32)
+    for s in range(slots):
+        block = traces[:, s, :] * present * signs[s]
+        tm[0:modes, sl(s)] = block
+        nm_src[s, 0:modes, :] = block
+        full = nm_src[s]
+        z = images[:, s, :]
+        d = dirs[:, s, :]
+        if koff > stored:
+            z = jnp.concatenate([z, zero_rows], axis=0)
+            d = jnp.concatenate([d, zero_rows], axis=0)
+        zh, zl = split(z)
+        z_hi[:, sl(s)] = zh
+        z_lo[:, sl(s)] = zl
+        kz = kz + mmf(full, z, 1, 1)
+        kd = kd + mmf(full, d, 1, 1)
+        parts = [jnp.zeros((koff, face), F32), d]
+        if kw > 2 * koff:
+            parts.append(jnp.zeros((kw - 2 * koff, face), F32))
+        dt = jnp.concatenate(parts, axis=0).T
+        dh, dl = split(dt)
+        xd_hi[sl(s), :] = dh
+        xd_lo[sl(s), :] = dl
+    th, tl = split(tm[...])
+    t_hi[...] = th
+    t_lo[...] = tl
+    g_src[:, npad + rhs:npad + rhs + koff] = kz
+    g_src[:, npad + rhs + koff:npad + rhs + 2 * koff] = kd
+    g_dst[me] = g_src[...]
+
+    pl.semaphore_wait(barrier, n - 1)
+    peers(lambda e: to_peer(g_src, g_dst, g_ss, g_rs, e).start())
+    for s in range(slots):
+        to_face(nm_src, nm_dst, nm_ss, nm_rs, s).start()
+
+    for s in range(slots):
+        rows = lax.broadcasted_iota(jnp.int32, (face, nb), 0) + s * face
+        perm[sl(s), :] = jnp.where(rows == bmap[...], signs[s], 0.0).astype(BF16)
+    fhi, flo = split(flex[...])
+
+    for s in range(slots):
+        p = perm[sl(s), :]
+        a_hi[sl(s), :] = mm(mm(p, fhi).astype(BF16), perm[...], 1, 1).astype(BF16)
+        a_lo[sl(s), :] = mm(mm(p, flo).astype(BF16), perm[...], 1, 1).astype(BF16)
+
+    for s in range(slots):
+        to_face(nm_src, nm_dst, nm_ss, nm_rs, s).wait()
+    peers(lambda e: from_peer(g_src, g_dst, g_ss, g_rs, e).wait())
+
+    cg = g_dst[:, :, 0:npad].reshape(npad, npad)
+    load = g_dst[:, :, npad:npad + rhs].reshape(npad, rhs)
+    kg = g_dst[:, :, npad + rhs:].reshape(npad, kw)
+    for s in range(slots):
+        own = mmf(nm_src[s], g_src[:, 0:npad], 0, 0)
+        other = mmf(nm_dst[s], g_dst[linear(neighbour(s))][:, 0:npad], 0, 0)
+        mh, ml = split(own + other)
+        m_hi[sl(s), :] = mh
+        m_lo[sl(s), :] = ml
+    mh, ml = split(mmf(kg, cg, 0, 0))
+    m_hi[nb:nb + kw, :] = mh
+    m_lo[nb:nb + kw, :] = ml
+    mh, ml = split(cg)
+    m_hi[nb + kw:, :] = mh
+    m_lo[nb + kw:, :] = ml
+    xh, xl = split(mmf(cg, kg))
+    xd_hi[nb:, :] = xh
+    xd_lo[nb:, :] = xl
+
+    lp, lh = pair(load)
+    lam0 = dot3(m_hi[0:nb, :], m_lo[0:nb, :], lp, lh)
+    for s in range(slots):
+        lam[s] = lam0[sl(s), :]
+    bc_src[...] = jnp.zeros_like(bc_src)
+    rs_src[...] = jnp.zeros_like(rs_src)
+
+    def advance(field, extras, first):
+        fp, fh = pair(field)
+        acc = [[] for _ in extras]
+        for s in range(slots):
+            h = dot3(a_hi[sl(s), :], a_lo[sl(s), :], fp, fh)
+            if first:
+                h = disp[s] * signs[s] - h
+            hbuf[s] = h
+            to_face(hbuf, fbuf, f_ss, f_rs, s).start()
+        hall = hbuf[...].reshape(nb, rhs)
+        hp, hh = pair(hall)
+        zh = dot3(z_hi[...], z_lo[...], hp, hh)
+        rows = [zh]
+        count = koff
+        for u, v in extras:
+            rows.append(colsum(u * (hall if v is None else v)))
+            count += 1
+        if chunk * n > count:
+            rows.append(jnp.zeros((chunk * n - count, rhs), F32))
+        full = jnp.concatenate(rows, axis=0)
+        for j in range(chunk):
+            rs_src[:, j, :] = full[j * n:(j + 1) * n]
+        rs_dst[me] = rs_src[me]
+        peers(lambda e: to_peer(rs_src.at[e], rs_dst, rs_ss, rs_rs, e).start())
+        for s in range(slots):
+            to_face(hbuf, fbuf, f_ss, f_rs, s).wait()
+        y = hall + fbuf[...].reshape(nb, rhs)
+        ybuf[...] = y
+        yy = colsum(hall * y)
+        yp, yh = pair(y)
+        c_own = dot3(t_hi[...], t_lo[...], yp, yh)
+        bc_src[0:mp, :] = c_own
+        bc_src[mp:mp + 1, :] = yy
+        peers(lambda e: from_peer(rs_src.at[e], rs_dst, rs_ss, rs_rs, e).wait())
+        bc_src[mp + 1:mp + 1 + chunk, :] = jnp.sum(rs_dst[...], axis=0)
+        bc_dst[me] = bc_src[...]
+        peers(lambda e: to_peer(bc_src, bc_dst, bc_ss, bc_rs, e).start())
+        peers(lambda e: from_peer(bc_src, bc_dst, bc_ss, bc_rs, e).wait())
+        got = bc_dst[...]
+        c = got[:, 0:mp, :].reshape(npad, rhs)
+        yy = jnp.sum(got[:, mp, :], axis=0, keepdims=True)
+        totals = jnp.concatenate([got[:, mp + 1 + j, :] for j in range(chunk)], axis=0)
+        cp, ch = pair(c)
+        res = dot3(m_hi[...], m_lo[...], cp, ch)
+        image = ybuf[...] - res[0:nb]
+        zq = totals[0:koff] - res[nb:nb + koff]
+        alpha = res[nb + kw:]
+        ex = [totals[koff + i:koff + i + 1] for i in range(len(extras))]
+        return image, zq, ex, yy, c, alpha
+
+    image, zw, _, _, _, _ = advance(lam0, [], True)
+    w_now = image
+    curve_inv = 1.0 / curv[...]
+    qw = []
+    curves = []
+    for k in range(ITERS):
+        beta = zw * curve_inv
+        parts = [jnp.zeros((koff, rhs), F32), beta]
+        if kw > 2 * koff:
+            parts.append(jnp.zeros((kw - 2 * koff, rhs), F32))
+        bp, bh = pair(jnp.concatenate(parts, axis=0))
+        sub = dot3(xd_hi[...], xd_lo[...], bp, bh)
+        p = w_now - sub[0:nb]
+        v = -sub[nb:]
+        for j in range(k):
+            gamma = qw[j] / curves[j]
+            p = p - pbuf[j] * gamma
+            v = v - vbuf[j] * gamma
+        half = (lax.broadcasted_iota(jnp.int32, (nb, rhs), 0) // face) % 2
+        extras = [(p, None), (w_now, None), (jnp.where(half == 1, p, 0.0), w_now)]
+        extras += [(qbuf[j], None) for j in range(k)]
+        image, zq, ex, yy, c, alpha = advance(p, extras, False)
+        pq = ex[0] - colsum(v * c)
+        rate = ex[2] / pq
+        plain = rate * p
+        for s in range(slots):
+            lam[s] = lam[s] + plain[sl(s), :]
+        if k + 1 < ITERS:
+            pbuf[k] = p
+            qbuf[k] = image
+            vbuf[k] = v
+            curves.append(pq)
+            qw = [qw[j] - rate * ex[3 + j] for j in range(k)]
+            qw.append(ex[1] - rate * (yy - colsum(c * alpha)))
+            zw = zw - rate * zq
+        w_now = w_now - rate * image
+    for s in range(slots):
+        w[s] = w_now[sl(s), :]
+
+
+def per_device(sizes, local_displacement, coarse_load, flexibility, block_map, mode_counts,
+               mode_traces, coarse_rows, stored_dirs, stored_images, stored_curv):
+    n = sizes[0] * sizes[1] * sizes[2]
+    disp = local_displacement[0, 0, 0]
+    slots, face, rhs = disp.shape
+    nb = slots * face
+    traces = mode_traces[0, 0, 0]
+    modes = traces.shape[0]
+    stored = stored_dirs.shape[3]
+    mp = up_to(modes, 8)
+    npad = n * mp
+    koff = up_to(stored, 8)
+    kw = up_to(2 * koff, 128)
+    chunk = -(-(koff + 3 + ITERS) // n)
+    rows = jnp.pad(coarse_rows[0, 0, 0].reshape(modes, n, modes),
+                   ((0, mp - modes), (0, 0), (0, mp - modes))).reshape(mp, npad)
+    small = jnp.concatenate([rows, jnp.pad(coarse_load[0, 0, 0], ((0, mp - modes), (0, 0)))], axis=1)
+    curv = jnp.pad(stored_curv, (0, koff - stored), constant_values=1.0)[:, None]
+    width = npad + rhs + kw
+    brow = up_to(mp + 1 + chunk, 8)
+    vm = pl.BlockSpec(memory_space=pltpu.VMEM)
+    sem = pltpu.SemaphoreType.DMA
+    out = jax.ShapeDtypeStruct((slots, face, rhs), F32)
+    lam, resid = pl.pallas_call(
+        functools.partial(kernel, sizes),
+        out_shape=(out, out),
+        in_specs=[vm, vm, vm, vm, pl.BlockSpec(memory_space=pltpu.SMEM), vm, vm, vm, vm],
+        out_specs=(vm, vm),
+        scratch_shapes=[
+            pltpu.VMEM((nb, nb), BF16),
+            pltpu.VMEM((nb, nb), BF16), pltpu.VMEM((nb, nb), BF16),
+            pltpu.VMEM((nb + kw + npad, npad), BF16), pltpu.VMEM((nb + kw + npad, npad), BF16),
+            pltpu.VMEM((nb + npad, kw), BF16), pltpu.VMEM((nb + npad, kw), BF16),
+            pltpu.VMEM((koff, nb), BF16), pltpu.VMEM((koff, nb), BF16),
+            pltpu.VMEM((mp, nb), F32), pltpu.VMEM((mp, nb), BF16), pltpu.VMEM((mp, nb), BF16),
+            pltpu.VMEM((mp, width), F32), pltpu.VMEM((n, mp, width), F32),
+            pltpu.VMEM((slots, mp, face), F32), pltpu.VMEM((slots, mp, face), F32),
+            pltpu.VMEM((slots, face, rhs), F32), pltpu.VMEM((slots, face, rhs), F32),
+            pltpu.VMEM((nb, rhs), F32),
+            pltpu.VMEM((n, chunk, rhs), F32), pltpu.VMEM((n, chunk, rhs), F32),
+            pltpu.VMEM((brow, rhs), F32), pltpu.VMEM((n, brow, rhs), F32),
+            pltpu.VMEM((ITERS - 1, nb, rhs), F32), pltpu.VMEM((ITERS - 1, nb, rhs), F32),
+            pltpu.VMEM((ITERS - 1, npad, rhs), F32),
+            sem((n,)), sem((n,)), sem((slots,)), sem((slots,)), sem((slots,)), sem((slots,)),
+            sem((n,)), sem((n,)), sem((n,)), sem((n,)),
+        ],
+        compiler_params=pltpu.CompilerParams(
+            collective_id=0, has_side_effects=True, vmem_limit_bytes=67043328),
+    )(disp, small, flexibility[0, 0, 0], block_map[0, 0], mode_counts[0, 0], traces,
+      stored_dirs[0, 0, 0], stored_images[0, 0, 0], curv)
+    return lam[None, None, None], resid[None, None, None]
 
 
 def extended(x, sides, width):
@@ -45,16 +371,16 @@
 
 
 def stored_inner(store, field):
-    return jnp.einsum("isf,sfr->ir", store[:, 1::2], field[1::2], precision=precise)
+    return jnp.einsum("isf,sfr->ir", store[:, 1::2], field[1::2], precision=lax.Precision.HIGHEST)
 
 
 def coarse_solve(loads, rows):
     return jnp.dot(
-        rows, lax.all_gather(loads, ("gx", "gy", "gz"), axis=0, tiled=True), precision=precise
+        rows, lax.all_gather(loads, ("gx", "gy", "gz"), axis=0, tiled=True), precision=lax.Precision.HIGHEST
     )
 
 
-def per_device(
+def per_device_plain(
     local_displacement,
     coarse_load,
     flexibility,
@@ -73,7 +399,7 @@
     rows = coarse_rows[0, 0, 0]
     dirs_store = stored_dirs[0, 0, 0]
     images_store = stored_images[0, 0, 0]
-    signs = jnp.array(slot_signs, jnp.float32)
+    signs = jnp.array((-1.0, 1.0, -1.0, 1.0, -1.0, 1.0), jnp.float32)
     field_signs = signs[:, None, None]
     nmodes = mode_traces.shape[3]
     present = (jnp.arange(nmodes, dtype=jnp.int32) < mode_counts[0, 0, 0]).astype(jnp.float32)
@@ -85,13 +411,13 @@
 
     def operate(field):
         flat = (field_signs * field).reshape(size_nb, layout[2])
-        return jnp.dot(flex_face, flat, precision=precise).reshape(layout)
+        return jnp.dot(flex_face, flat, precision=lax.Precision.HIGHEST).reshape(layout)
 
     def graph(alpha):
-        return assemble(jnp.einsum("msf,mr->sfr", signed, alpha, precision=precise))
+        return assemble(jnp.einsum("msf,mr->sfr", signed, alpha, precision=lax.Precision.HIGHEST))
 
     def project(field):
-        partial_loads = jnp.einsum("msf,sfr->mr", signed, field, precision=precise)
+        partial_loads = jnp.einsum("msf,sfr->mr", signed, field, precision=lax.Precision.HIGHEST)
         return field - graph(coarse_solve(partial_loads, rows))
 
     lam = graph(coarse_solve(loads, rows))
@@ -103,10 +429,10 @@
             own_rows = jnp.stack([plus_inner(images[index], resid) for index in range(len(images))])
             local_rows = jnp.concatenate([local_rows, own_rows], axis=0)
         totals = lax.psum(local_rows, ("gx", "gy", "gz"))
-        beta = totals[:STORED] / stored_curv[:, None]
-        direction = resid - jnp.einsum("isf,ir->sfr", dirs_store, beta, precision=precise)
+        beta = totals[:stored_curv.shape[0]] / stored_curv[:, None]
+        direction = resid - jnp.einsum("isf,ir->sfr", dirs_store, beta, precision=lax.Precision.HIGHEST)
         for index in range(len(directions)):
-            direction = direction - directions[index] * (totals[STORED + index] / curves[index])
+            direction = direction - directions[index] * (totals[stored_curv.shape[0] + index] / curves[index])
         image_now = project(assemble(field_signs * operate(direction)))
         pair = lax.psum(
             jnp.stack([plus_inner(direction, image_now), plus_inner(direction, resid)]),
@@ -122,21 +448,18 @@
 
 
 def solution(mesh):
-    return jax.shard_map(
-        per_device,
-        mesh=mesh,
-        in_specs=(
-            P("gx", "gy", "gz", None, None, None),
-            P("gx", "gy", "gz", None, None),
-            P("gx", "gy", "gz", None, None),
-            P("gx", "gy", "gz", None),
-            P("gx", "gy", "gz"),
-            P("gx", "gy", "gz", None, None, None),
-            P("gx", "gy", "gz", None, None),
-            P("gx", "gy", "gz", None, None, None),
-            P("gx", "gy", "gz", None, None, None),
-            P(),
-        ),
-        out_specs=(P("gx", "gy", "gz", None, None, None), P("gx", "gy", "gz", None, None, None)),
-        check_vma=False,
-    )
+    sizes = tuple(mesh.shape[a] for a in AXES)
+    grid = P(*AXES)
+
+    def program(*args):
+        coarse = sizes[0] * sizes[1] * sizes[2] * up_to(args[5].shape[3], 8)
+        one = functools.partial(per_device, sizes) if coarse <= 512 else per_device_plain
+        return jax.shard_map(
+            one,
+            mesh=mesh,
+            in_specs=(grid,) * 9 + (P(),),
+            out_specs=(grid, grid),
+            check_vma=False,
+        )(*args)
+
+    return program

time: 668 us -> 106 us (0.16)
  blocking collectives: 440 us -> 0 us
  Pallas kernels: 0 us -> 94.2 us
  starting transfers between devices: 64.8 us -> 0 us
  other arithmetic: 60.4 us -> 1.31 us
  matrix products: 34.5 us -> 0 us
  waiting for transfers between devices: 32.7 us -> 0 us
  local copies, waits for them, and re-layouts: 29.8 us -> 8.86 us
    psum x6 -> x0, blocking collectives: 234 us -> none  [the longest x3 122 us: per_device(): totals = lax.psum(local_rows, ('gx', 'gy', 'gz'))]
    all_gather x5 -> x0, blocking collectives: 206 us -> none  [coarse_solve(): lax.all_gather(loads, ('gx', 'gy', 'gz'), axis=0, tiled=True)]
    pallas_call x0 -> x1, Pallas kernels: none -> 94.2 us  [per_device(): pl.pallas_call(functools.partial(kernel, sizes), out_shape=(out, out), in...]
    ppermute x54 -> x0, starting transfers between devices: 64.8 us -> none  [the longest x27 45.3 us: extended(): after = lax.ppermute(initial, axis, down)]
    dot_general x24 -> x0, matrix products: 34.5 us -> none  [the longest x4 14.8 us: operate(): return jnp.dot(flex_face, flat, precision=precise).reshape(layout)]
    ppermute x54 -> x0, waiting for transfers between devices: 32.7 us -> none  [the longest x27 20.6 us: extended(): after = lax.ppermute(initial, axis, down)]
    unnamed x76 -> x1, other arithmetic: 32.8 us -> 0.71 us
    gather x2 -> x0, local copies, waits for them, and re-layouts: 9.22 us -> none  [per_device(): flex_face = jnp.take(jnp.take(flex, inverse, axis=0), inverse, axis=1)]
  transfers between devices with their start and end apart: 54 -> 0, of which waited for: 13 -> 0; matrix products, arithmetic and copies ran while one was open for 9% -> 0% of each run, Pallas kernels for 0% -> 0%
where the time goes in v1:
time: 106 us
  Pallas kernels  94.2 us (89%)
  local copies, waits for them, and re-layouts  8.86 us (8%)
  other arithmetic  1.31 us (1%)
  between operations  1.31 us (1%)
    pallas_call x1, Pallas kernels, per_device(): pl.pallas_call(functools.partial(kernel, sizes), out_shape=(out, out), in...  94.2 us
    unnamed x4, local copies, waits for them, and re-layouts  5.54 us

profile of v1, /device:TPU:0, one launch (start us, length us, event | category | flops | bytes accessed | tf_op | source)
XLA Modules:
  0.0 105.7 jit_solution(17131448337565349307)
XLA Ops:
  1.3 0.7 copy.25
  2.0 0.7 reduce
  2.7 1.3 %copy.17.curv = f32[40,1]{1,0:T(8,128)} copy(f32[40,1]{0,1:T(1,128)} %bitcast.25) | data formatting | bytes 320 | tf_op jit(solution)/shard_map/broadcast_in_dim | solution.py:304
  4.0 1.3 %copy.24 = f32[1,1,1,6,6,128]{5,4,2,3,1,0:T(8,128)} copy(f32[1,1,1,6,6,128]{5,2,4,3,1,0:T(1,128)} %param.15) | data formatting | bytes 36864
  5.3 0.1 reshape_squeeze.3
  5.5 0.1 reshape.7
  5.6 0.6 select_maximum_fusion.small
  6.2 1.7 %copy_bitcast_fusion = (f32[40,6,128]{2,1,0:T(8,128)}, f32[40,6,128]{2,1,0:T(8,128)}) fusion(f32[1,1,1,40,6,128]{5,3,4,2,1,0:T(8,128)} %param.18, f32[1,1,1,40,6,128]{5,3,4,2,1,0:T(8,128)} %param.17), kind=kLoop, calls=%fused_computation | loop fusion | bytes 491520 | tf_op jit(solution)/shard_map/squeeze | solution.py:336
  7.9 94.2 %shard_map.113 = (f32[6,128,128]{2,1,0:T(8,128)}, f32[6,128,128]{2,1,0:T(8,128)}) custom-call(f32[6,128,128]{2,1,0:T(8,128)} %bitcast.21, f32[8,384]{1,0:T(8,128)} %select_maximum_fusion.small, f32[768,768]{1,0:T(8,128)} %bitcast.18, s32[1,768]{1,0:T(1,128)} %bitcast.24, s32[1]{0:T(128)} %bitcast.17.cnt, f32[6,6,128]{2,1,0:T(8,128)} %bitcast.22, ...), custom_call_target="tpu_custom_call" | custom-call | tf_op jit(solution)/shard_map/pallas_call | solution.py:310
  102.2 1.8 %copy.29 = f32[1,1,1,6,128,128]{5,4,3,2,1,0:T(8,128)} copy(f32[1,1,1,6,128,128]{5,4,3,2,1,0:T(8,128)} %bitcast.20) | data formatting | bytes 786432
  103.9 1.8 %copy.30 = f32[1,1,1,6,128,128]{5,4,3,2,1,0:T(8,128)} copy(f32[1,1,1,6,128,128]{5,4,3,2,1,0:T(8,128)} %bitcast.19) | data formatting | bytes 786432
  (1 shorter events, 0.0 us)

commit v2 on v1

--- a/solution.py
+++ b/solution.py
@@ -50,19 +50,19 @@
 
 def kernel(
     sizes,
-    disp, small, flex, bmap, cnt, traces, dirs, images, curv,
+    disp, rows_in, load_in, flex, bmap, cnt, traces, dirs, images, curv,
     lam, w,
     perm, a_hi, a_lo, m_hi, m_lo, xd_hi, xd_lo, z_hi, z_lo, tm, t_hi, t_lo,
-    g_src, g_dst, nm_src, nm_dst, hbuf, fbuf, ybuf, rs_src, rs_dst, bc_src, bc_dst,
+    g_src, g_dst, l_src, l_dst, nm_src, nm_dst, hbuf, fbuf, ybuf, rs_src, rs_dst, bc_src, bc_dst,
     pbuf, qbuf, vbuf,
-    g_ss, g_rs, nm_ss, nm_rs, f_ss, f_rs, rs_ss, rs_rs, bc_ss, bc_rs,
+    g_ss, g_rs, l_ss, l_rs, nm_ss, nm_rs, f_ss, f_rs, rs_ss, rs_rs, bc_ss, bc_rs,
 ):
     nx, ny, nz = sizes
     n = nx * ny * nz
     slots, face, rhs = disp.shape
     nb = slots * face
-    stored = dirs.shape[0]
-    modes = traces.shape[0]
+    stored = dirs.shape[1]
+    modes = load_in.shape[0]
     mp = tm.shape[0]
     npad = n * mp
     koff = up_to(stored, 8)
@@ -71,8 +71,17 @@
     cx, cy, cz = (lax.axis_index(a) for a in AXES)
     me = (cx * ny + cy) * nz + cz
 
-    def coords(e):
-        return (e // (ny * nz), (e // nz) % ny, e % nz)
+    here = (cx, cy, cz)
+    plus = [[lax.rem(c + d, size) for d in range(size)] for c, size in zip(here, sizes)]
+    minus = [[lax.rem(c + size - d, size) for d in range(size)] for c, size in zip(here, sizes)]
+    offsets = [(i, j, l) for i in range(nx) for j in range(ny) for l in range(nz)][1:]
+    offsets.sort(key=lambda o: -sum(min(d, size - d) for d, size in zip(o, sizes)))
+
+    def target(o):
+        return tuple(plus[a][o[a]] for a in range(3))
+
+    def origin(o):
+        return tuple(minus[a][o[a]] for a in range(3))
 
     def neighbour(slot):
         c = [cx, cy, cz]
@@ -88,20 +97,13 @@
         return slice(s * face, (s + 1) * face)
 
     def peers(body):
-        def step(r, carry):
-            body(lax.rem(me + r, n))
-            return carry
-        lax.fori_loop(1, n, step, 0)
-
-    def to_peer(src, dst, ss, rs, e):
+        for r, o in enumerate(offsets):
+            body(r, o)
+
+    def to_peer(src, dst, ss, rs, r, o):
         return pltpu.make_async_remote_copy(
-            src_ref=src, dst_ref=dst.at[me], send_sem=ss.at[e], recv_sem=rs.at[me],
-            device_id=coords(e), device_id_type=MESH)
-
-    def from_peer(src, dst, ss, rs, e):
-        return pltpu.make_async_remote_copy(
-            src_ref=src, dst_ref=dst.at[e], send_sem=ss.at[e], recv_sem=rs.at[e],
-            device_id=coords(e), device_id_type=MESH)
+            src_ref=src, dst_ref=dst, send_sem=ss.at[r], recv_sem=rs.at[r],
+            device_id=target(o), device_id_type=MESH)
 
     def to_face(src, dst, ss, rs, s):
         return pltpu.make_async_remote_copy(
@@ -109,24 +111,32 @@
             device_id=neighbour(s), device_id_type=MESH)
 
     barrier = pltpu.get_barrier_semaphore()
-    peers(lambda e: pl.semaphore_signal(barrier, inc=1, device_id=coords(e), device_id_type=MESH))
+    peers(lambda r, o: pl.semaphore_signal(
+        barrier, inc=1, device_id=target(o), device_id_type=MESH))
 
     signs = [-1.0, 1.0] * (slots // 2)
-    present = (lax.broadcasted_iota(jnp.int32, (modes, face), 0) < cnt[0]).astype(F32)
+    present = (lax.broadcasted_iota(jnp.int32, (modes, face), 0) < cnt[...]).astype(F32)
     tm[...] = jnp.zeros_like(tm)
     nm_src[...] = jnp.zeros_like(nm_src)
-    g_src[:, npad + rhs:] = jnp.zeros((mp, kw), F32)
-    g_src[:, :npad + rhs] = small[...]
+    g_src[...] = jnp.zeros_like(g_src)
+    l_src[...] = jnp.zeros_like(l_src)
+    l_src[0:modes, :] = load_in[:, 0, :]
+    wide = lax.broadcasted_iota(jnp.int32, (n * modes, npad), 1)
+    tall = lax.broadcasted_iota(jnp.int32, (n * modes, npad), 0)
+    spread = (wide // mp * modes + wide % mp == tall) & (wide % mp < modes)
+    g_src[0:modes, 0:npad] = mmf(rows_in[:, 0, :], spread.astype(F32))
     kz = jnp.zeros((mp, koff), F32)
     kd = jnp.zeros((mp, koff), F32)
     zero_rows = jnp.zeros((koff - stored, face), F32)
     for s in range(slots):
-        block = traces[:, s, :] * present * signs[s]
+        block = jnp.concatenate([traces[m * slots + s] for m in range(modes)], axis=0)
+        block = block * present * signs[s]
         tm[0:modes, sl(s)] = block
-        nm_src[s, 0:modes, :] = block
-        full = nm_src[s]
-        z = images[:, s, :]
-        d = dirs[:, s, :]
+        nm_src[s, 0:modes, npad:] = block
+        nm_src[s, :, 0:npad] = g_src[:, 0:npad]
+        full = nm_src[s, :, npad:]
+        z = images[s]
+        d = dirs[s]
         if koff > stored:
             z = jnp.concatenate([z, zero_rows], axis=0)
             d = jnp.concatenate([d, zero_rows], axis=0)
@@ -145,18 +155,20 @@
     th, tl = split(tm[...])
     t_hi[...] = th
     t_lo[...] = tl
-    g_src[:, npad + rhs:npad + rhs + koff] = kz
-    g_src[:, npad + rhs + koff:npad + rhs + 2 * koff] = kd
+    g_src[:, npad:npad + koff] = kz
+    g_src[:, npad + koff:npad + 2 * koff] = kd
     g_dst[me] = g_src[...]
-
-    pl.semaphore_wait(barrier, n - 1)
-    peers(lambda e: to_peer(g_src, g_dst, g_ss, g_rs, e).start())
-    for s in range(slots):
-        to_face(nm_src, nm_dst, nm_ss, nm_rs, s).start()
-
+    l_dst[me] = l_src[...]
     for s in range(slots):
         rows = lax.broadcasted_iota(jnp.int32, (face, nb), 0) + s * face
         perm[sl(s), :] = jnp.where(rows == bmap[...], signs[s], 0.0).astype(BF16)
+
+    pl.semaphore_wait(barrier, n - 1)
+    peers(lambda r, o: to_peer(l_src, l_dst.at[me], l_ss, l_rs, r, o).start())
+    for s in range(slots):
+        to_face(nm_src, nm_dst, nm_ss, nm_rs, s).start()
+    peers(lambda r, o: to_peer(g_src, g_dst.at[me], g_ss, g_rs, r, o).start())
+
     fhi, flo = split(flex[...])
 
     for s in range(slots):
@@ -166,26 +178,29 @@
 
     for s in range(slots):
         to_face(nm_src, nm_dst, nm_ss, nm_rs, s).wait()
-    peers(lambda e: from_peer(g_src, g_dst, g_ss, g_rs, e).wait())
-
-    cg = g_dst[:, :, 0:npad].reshape(npad, npad)
-    load = g_dst[:, :, npad:npad + rhs].reshape(npad, rhs)
-    kg = g_dst[:, :, npad + rhs:].reshape(npad, kw)
-    for s in range(slots):
-        own = mmf(nm_src[s], g_src[:, 0:npad], 0, 0)
-        other = mmf(nm_dst[s], g_dst[linear(neighbour(s))][:, 0:npad], 0, 0)
+    peers(lambda r, o: to_peer(l_src, l_dst.at[linear(origin(o))], l_ss, l_rs, r, o).wait())
+
+    load = l_dst[...].reshape(npad, rhs)
+    for s in range(slots):
+        own = mmf(nm_src[s, :, npad:], g_src[:, 0:npad], 0, 0)
+        other = mmf(nm_dst[s, :, npad:], nm_dst[s, :, 0:npad], 0, 0)
         mh, ml = split(own + other)
         m_hi[sl(s), :] = mh
         m_lo[sl(s), :] = ml
-    mh, ml = split(mmf(kg, cg, 0, 0))
-    m_hi[nb:nb + kw, :] = mh
-    m_lo[nb:nb + kw, :] = ml
-    mh, ml = split(cg)
-    m_hi[nb + kw:, :] = mh
-    m_lo[nb + kw:, :] = ml
-    xh, xl = split(mmf(cg, kg))
-    xd_hi[nb:, :] = xh
-    xd_lo[nb:, :] = xl
+
+    def finish_setup():
+        peers(lambda r, o: to_peer(g_src, g_dst.at[linear(origin(o))], g_ss, g_rs, r, o).wait())
+        cg = g_dst[:, :, 0:npad].reshape(npad, npad)
+        kg = g_dst[:, :, npad:].reshape(npad, kw)
+        mh, ml = split(mmf(kg, cg, 0, 0))
+        m_hi[nb:nb + kw, :] = mh
+        m_lo[nb:nb + kw, :] = ml
+        mh, ml = split(cg)
+        m_hi[nb + kw:, :] = mh
+        m_lo[nb + kw:, :] = ml
+        xh, xl = split(mmf(cg, kg))
+        xd_hi[nb:, :] = xh
+        xd_lo[nb:, :] = xl
 
     lp, lh = pair(load)
     lam0 = dot3(m_hi[0:nb, :], m_lo[0:nb, :], lp, lh)
@@ -194,9 +209,8 @@
     bc_src[...] = jnp.zeros_like(bc_src)
     rs_src[...] = jnp.zeros_like(rs_src)
 
-    def advance(field, extras, first):
+    def advance(field, extras, first, last=False):
         fp, fh = pair(field)
-        acc = [[] for _ in extras]
         for s in range(slots):
             h = dot3(a_hi[sl(s), :], a_lo[sl(s), :], fp, fh)
             if first:
@@ -217,36 +231,48 @@
         for j in range(chunk):
             rs_src[:, j, :] = full[j * n:(j + 1) * n]
         rs_dst[me] = rs_src[me]
-        peers(lambda e: to_peer(rs_src.at[e], rs_dst, rs_ss, rs_rs, e).start())
+        peers(lambda r, o: to_peer(
+            rs_src.at[linear(target(o))], rs_dst.at[me], rs_ss, rs_rs, r, o).start())
+        if first:
+            finish_setup()
         for s in range(slots):
             to_face(hbuf, fbuf, f_ss, f_rs, s).wait()
         y = hall + fbuf[...].reshape(nb, rhs)
         ybuf[...] = y
-        yy = colsum(hall * y)
         yp, yh = pair(y)
         c_own = dot3(t_hi[...], t_lo[...], yp, yh)
         bc_src[0:mp, :] = c_own
-        bc_src[mp:mp + 1, :] = yy
-        peers(lambda e: from_peer(rs_src.at[e], rs_dst, rs_ss, rs_rs, e).wait())
-        bc_src[mp + 1:mp + 1 + chunk, :] = jnp.sum(rs_dst[...], axis=0)
+        squares = not (first or last)
+        fits = modes + chunk <= mp
+        if squares:
+            bc_src[mp:mp + 1, :] = colsum(hall * y)
+        at = modes if fits else mp + 1
+        used = mp + squares if fits else mp + 1 + chunk
+        peers(lambda r, o: to_peer(
+            rs_src.at[linear(target(o))], rs_dst.at[linear(origin(o))], rs_ss, rs_rs, r, o).wait())
+        bc_src[at:at + chunk, :] = jnp.sum(rs_dst[...], axis=0)
         bc_dst[me] = bc_src[...]
-        peers(lambda e: to_peer(bc_src, bc_dst, bc_ss, bc_rs, e).start())
-        peers(lambda e: from_peer(bc_src, bc_dst, bc_ss, bc_rs, e).wait())
-        got = bc_dst[...]
-        c = got[:, 0:mp, :].reshape(npad, rhs)
-        yy = jnp.sum(got[:, mp, :], axis=0, keepdims=True)
-        totals = jnp.concatenate([got[:, mp + 1 + j, :] for j in range(chunk)], axis=0)
+        part = bc_src.at[0:used]
+        peers(lambda r, o: to_peer(part, bc_dst.at[me, 0:used], bc_ss, bc_rs, r, o).start())
+        peers(lambda r, o: to_peer(
+            part, bc_dst.at[linear(origin(o)), 0:used], bc_ss, bc_rs, r, o).wait())
+        c = bc_dst[:, 0:mp, :].reshape(npad, rhs)
+        yy = jnp.sum(bc_dst[:, mp, :], axis=0, keepdims=True) if squares else None
+        totals = jnp.concatenate([bc_dst[:, at + j, :] for j in range(chunk)], axis=0)
         cp, ch = pair(c)
-        res = dot3(m_hi[...], m_lo[...], cp, ch)
+        need = nb if last else nb + kw if first else nb + kw + npad
+        res = dot3(m_hi[0:need, :], m_lo[0:need, :], cp, ch)
         image = ybuf[...] - res[0:nb]
-        zq = totals[0:koff] - res[nb:nb + koff]
-        alpha = res[nb + kw:]
+        zq = None if last else totals[0:koff] - res[nb:nb + koff]
+        alpha = res[nb + kw:] if squares else None
         ex = [totals[koff + i:koff + i + 1] for i in range(len(extras))]
         return image, zq, ex, yy, c, alpha
 
     image, zw, _, _, _, _ = advance(lam0, [], True)
     w_now = image
-    curve_inv = 1.0 / curv[...]
+    square = (koff, koff)
+    eye = lax.broadcasted_iota(jnp.int32, square, 0) == lax.broadcasted_iota(jnp.int32, square, 1)
+    curve_inv = 1.0 / jnp.sum(jnp.where(eye, curv[...], 0.0), axis=1, keepdims=True)
     qw = []
     curves = []
     for k in range(ITERS):
@@ -265,7 +291,7 @@
         half = (lax.broadcasted_iota(jnp.int32, (nb, rhs), 0) // face) % 2
         extras = [(p, None), (w_now, None), (jnp.where(half == 1, p, 0.0), w_now)]
         extras += [(qbuf[j], None) for j in range(k)]
-        image, zq, ex, yy, c, alpha = advance(p, extras, False)
+        image, zq, ex, yy, c, alpha = advance(p, extras, False, k + 1 == ITERS)
         pq = ex[0] - colsum(v * c)
         rate = ex[2] / pq
         plain = rate * p
@@ -290,19 +316,16 @@
     disp = local_displacement[0, 0, 0]
     slots, face, rhs = disp.shape
     nb = slots * face
-    traces = mode_traces[0, 0, 0]
-    modes = traces.shape[0]
+    modes = mode_traces.shape[3]
+    traces = mode_traces.reshape(modes * slots, 1, face)
     stored = stored_dirs.shape[3]
     mp = up_to(modes, 8)
     npad = n * mp
     koff = up_to(stored, 8)
     kw = up_to(2 * koff, 128)
     chunk = -(-(koff + 3 + ITERS) // n)
-    rows = jnp.pad(coarse_rows[0, 0, 0].reshape(modes, n, modes),
-                   ((0, mp - modes), (0, 0), (0, mp - modes))).reshape(mp, npad)
-    small = jnp.concatenate([rows, jnp.pad(coarse_load[0, 0, 0], ((0, mp - modes), (0, 0)))], axis=1)
-    curv = jnp.pad(stored_curv, (0, koff - stored), constant_values=1.0)[:, None]
-    width = npad + rhs + kw
+    curv = jnp.pad(stored_curv, (0, koff - stored), constant_values=1.0)[None]
+    width = npad + kw
     brow = up_to(mp + 1 + chunk, 8)
     vm = pl.BlockSpec(memory_space=pltpu.VMEM)
     sem = pltpu.SemaphoreType.DMA
@@ -310,7 +333,7 @@
     lam, resid = pl.pallas_call(
         functools.partial(kernel, sizes),
         out_shape=(out, out),
-        in_specs=[vm, vm, vm, vm, pl.BlockSpec(memory_space=pltpu.SMEM), vm, vm, vm, vm],
+        in_specs=[vm] * 10,
         out_specs=(vm, vm),
         scratch_shapes=[
             pltpu.VMEM((nb, nb), BF16),
@@ -320,20 +343,22 @@
             pltpu.VMEM((koff, nb), BF16), pltpu.VMEM((koff, nb), BF16),
             pltpu.VMEM((mp, nb), F32), pltpu.VMEM((mp, nb), BF16), pltpu.VMEM((mp, nb), BF16),
             pltpu.VMEM((mp, width), F32), pltpu.VMEM((n, mp, width), F32),
-            pltpu.VMEM((slots, mp, face), F32), pltpu.VMEM((slots, mp, face), F32),
+            pltpu.VMEM((mp, rhs), F32), pltpu.VMEM((n, mp, rhs), F32),
+            pltpu.VMEM((slots, mp, npad + face), F32), pltpu.VMEM((slots, mp, npad + face), F32),
             pltpu.VMEM((slots, face, rhs), F32), pltpu.VMEM((slots, face, rhs), F32),
             pltpu.VMEM((nb, rhs), F32),
             pltpu.VMEM((n, chunk, rhs), F32), pltpu.VMEM((n, chunk, rhs), F32),
             pltpu.VMEM((brow, rhs), F32), pltpu.VMEM((n, brow, rhs), F32),
             pltpu.VMEM((ITERS - 1, nb, rhs), F32), pltpu.VMEM((ITERS - 1, nb, rhs), F32),
             pltpu.VMEM((ITERS - 1, npad, rhs), F32),
-            sem((n,)), sem((n,)), sem((slots,)), sem((slots,)), sem((slots,)), sem((slots,)),
+            sem((n,)), sem((n,)), sem((n,)), sem((n,)), sem((slots,)), sem((slots,)), sem((slots,)), sem((slots,)),
             sem((n,)), sem((n,)), sem((n,)), sem((n,)),
         ],
         compiler_params=pltpu.CompilerParams(
             collective_id=0, has_side_effects=True, vmem_limit_bytes=67043328),
-    )(disp, small, flexibility[0, 0, 0], block_map[0, 0], mode_counts[0, 0], traces,
-      stored_dirs[0, 0, 0], stored_images[0, 0, 0], curv)
+    )(disp, coarse_rows.reshape(modes, 1, n * modes), coarse_load.reshape(modes, 1, rhs),
+      flexibility[0, 0, 0], block_map[0, 0], mode_counts[0], traces,
+      jnp.swapaxes(stored_dirs[0, 0, 0], 0, 1), jnp.swapaxes(stored_images[0, 0, 0], 0, 1), curv)
     return lam[None, None, None], resid[None, None, None]
 
 

time: 106 us -> 81.1 us (0.77)
  Pallas kernels: 94.2 us -> 76.1 us
  local copies, waits for them, and re-layouts: 8.86 us -> 3.53 us
  other arithmetic: 1.31 us -> 0 us
    pallas_call x1, Pallas kernels: 94.2 us -> 76.1 us  [per_device(): pl.pallas_call(functools.partial(kernel, sizes), out_shape=(out, out), in...]
    unnamed x4 -> x2, local copies, waits for them, and re-layouts: 5.54 us -> 3.53 us
    squeeze x1 -> x0, local copies, waits for them, and re-layouts: 1.74 us -> none  [per_device(): stored_images[0, 0, 0]]
    broadcast_in_dim x1 -> x0, local copies, waits for them, and re-layouts: 1.33 us -> none  [per_device(): jnp.pad(stored_curv, (0, koff - stored), constant_values=1.0)[:, None]]
where the time goes in v2:
time: 81.1 us; the launch traced here: 80.9 us
  Pallas kernels  76.1 us (94%)
  local copies, waits for them, and re-layouts  3.53 us (4%)
  between operations  1.29 us (2%)
    pallas_call x1, Pallas kernels, per_device(): pl.pallas_call(functools.partial(kernel, sizes), out_shape=(out, out), in...  76.1 us
    unnamed x2, local copies, waits for them, and re-layouts  3.53 us

profile of v2, /device:TPU:0, one launch (start us, length us, event | category | flops | bytes accessed | tf_op | source)
XLA Modules:
  0.0 80.9 jit_solution(10659695106198482802)
XLA Ops:
  1.3 76.1 %shard_map.113 = (f32[6,128,128]{2,1,0:T(8,128)}, f32[6,128,128]{2,1,0:T(8,128)}) custom-call(f32[6,128,128]{2,1,0:T(8,128)} %bitcast.18, f32[6,1,192]{2,1,0:T(1,128)} %bitcast.24, f32[6,1,128]{2,1,0:T(1,128)} %bitcast.25, f32[768,768]{1,0:T(8,128)} %bitcast.17, s32[1,768]{1,0:T(1,128)} %bitcast.26, s32[1,1]{1,0:T(1,128)} %bitcast.16.cnt, ...), custom_call_target="tpu_custom_call" | custom-call | tf_op jit(solution)/shard_map/pallas_call | solution.py:333
  77.3 1.8 %copy.15 = f32[1,1,1,6,128,128]{5,4,3,2,1,0:T(8,128)} copy(f32[1,1,1,6,128,128]{5,4,3,2,1,0:T(8,128)} %bitcast.20) | data formatting | bytes 786432
  79.1 1.8 %copy.16 = f32[1,1,1,6,128,128]{5,4,3,2,1,0:T(8,128)} copy(f32[1,1,1,6,128,128]{5,4,3,2,1,0:T(8,128)} %bitcast.19) | data formatting | bytes 786432
